TPU v7x, 512 devices: a whole 4x8x8 slice. The times are simulated.
512 devices in a mesh: snode: 64 (over z, y), rows: 8 (over x, core).
Axes of the slice: x: 4, y: 8, z: 8, core: 2. Of those that a mesh axis runs over, the one named last changes fastest.
Arguments:
- anc_store: bfloat16 [8192, 8192], P('snode'), may hold values from -9 to 9
- patterns: int32 [64, 8], replicated, may hold values from 0 to 63, all different within a row
- tile_counts: int32 [64], replicated, may hold values from 1 to 8, 448 in all
- tile_owner: int32 [64], replicated, may hold values from 0 to 63, as said below
- l_offdiag: bfloat16 [65536, 512], P(('snode', 'rows')), may hold values from -0.25 to 0.25
- diag_inverse: bfloat16 [32768, 512], P(('snode', 'rows')), may hold values from -1 to 2, as said below
Outputs:
- sigma_offdiag: bfloat16 [65536, 512], P(('snode', 'rows'))
- sigma_diag: float32 [32768, 512], P(('snode', 'rows'))
Inputs may be any that keep to these rules, and one draw needn't show every extreme that they name: `patterns`: each supernode's row names 8 different ancestor tiles. Slots before tile_counts[s] of a supernode's pattern are live, the rest padding; some supernode has all 8 slots live. `tile_owner`: a permutation of the ancestor tiles. `diag_inverse`: each supernode's block of 512 rows is lower triangular with diagonal entries between 1 and 2.
All inputs are finite; a program needn't handle non-finite values.
Results may differ from a plain program's by a relative error of at most 0.014.
Values may be sent and summed in bfloat16 or wider, within the bound.
A program may use at most 64 MiB of HBM per device.

v0:
```python
import jax
import jax.numpy as jnp
from jax import lax
from jax.sharding import PartitionSpec as P


def row_block(matrix, index):
    return lax.dynamic_index_in_dim(matrix, index, 0, keepdims=False)


def per_device(anc_store, patterns, tile_counts, tile_owner, l_offdiag, diag_inverse):
    tile_rows = anc_store.shape[0]
    pool_size = tile_owner.shape[0]
    group_count = patterns.shape[0]
    pattern_len = patterns.shape[1]
    group_id = lax.axis_index("snode")
    part_id = lax.axis_index("rows")
    local_tiles = l_offdiag.shape[0] // tile_rows
    band_rows = diag_inverse.shape[0]
    band_start = part_id * band_rows
    live_mask = jnp.arange(pattern_len, dtype=jnp.int32)[None, :] < tile_counts[:, None]
    own_live = lax.dynamic_slice_in_dim(
        row_block(live_mask, group_id), part_id * local_tiles, local_tiles
    )
    keep_rows = jnp.repeat(own_live, tile_rows)
    masked_l = jnp.where(keep_rows[:, None], l_offdiag, jnp.zeros_like(l_offdiag))
    piece = lax.all_gather(diag_inverse, "rows", axis=0, tiled=True)
    u_total = jnp.dot(masked_l, piece, preferred_element_type=jnp.float32)
    own_cols = lax.dynamic_slice_in_dim(piece, band_start, band_rows, 1)
    d_total = lax.dot_general(
        own_cols, piece, (((0,), (0,)), ((), ())), preferred_element_type=jnp.float32
    )
    u_total, base_diag = (u_total, d_total)
    u_factor = u_total.astype(jnp.bfloat16)
    owned_tile = jnp.sum(
        jnp.arange(pool_size, dtype=jnp.int32) * (tile_owner == group_id).astype(jnp.int32)
    )
    send_flag = jnp.any((patterns == owned_tile) & live_mask, axis=1)
    own_pattern = row_block(patterns, group_id)
    sources = jnp.take(tile_owner, own_pattern, axis=0)
    col_tiles = lax.dynamic_slice_in_dim(patterns, part_id * local_tiles, local_tiles, 1)
    stored_blocks = anc_store.reshape(tile_rows, pool_size, tile_rows)
    picked = jnp.take(stored_blocks, col_tiles, axis=1)
    picked = jnp.transpose(picked, (1, 0, 2, 3)).reshape(
        group_count, tile_rows, local_tiles * tile_rows
    )
    outgoing = jnp.where(send_flag[:, None, None], picked, jnp.zeros_like(picked))
    incoming = lax.all_to_all(outgoing, "snode", split_axis=0, concat_axis=0, tiled=True)
    arranged = jnp.take(incoming, sources, axis=0).reshape(
        pattern_len * tile_rows, local_tiles * tile_rows
    )
    own_rows = lax.all_to_all(arranged, "rows", split_axis=0, concat_axis=1, tiled=True)
    y_block = jnp.dot(
        own_rows,
        lax.all_gather(u_factor, "rows", axis=0, tiled=True),
        preferred_element_type=jnp.float32,
    )
    offdiag = (-y_block).astype(jnp.bfloat16)
    partial_diag = lax.dot_general(
        u_factor, offdiag, (((0,), (0,)), ((), ())), preferred_element_type=jnp.float32
    )
    whole_update = lax.psum(partial_diag.astype(jnp.bfloat16), "rows").astype(jnp.float32)
    reduced = lax.dynamic_slice_in_dim(whole_update, band_start, band_rows, 0)
    return (offdiag, base_diag - reduced)


def solution(mesh):
    in_specs = (
        P("snode", None),
        P(),
        P(),
        P(),
        P(("snode", "rows"), None),
        P(("snode", "rows"), None),
    )
    out_specs = (P(("snode", "rows"), None), P(("snode", "rows"), None))
    return jax.shard_map(
        per_device, mesh=mesh, in_specs=in_specs, out_specs=out_specs, check_vma=False
    )
```

profile of v0, /device:TPU:8, one launch (start us, length us, event | category | flops | bytes accessed | tf_op | source)
XLA Modules:
  0.0 179.3 jit_solution(5158815995826037886)
XLA Ops:
  7.2 0.7 and_bitcast_fusion
  7.9 3.2 %copy.8 = bf16[128,8192]{0,1:T(8,128)(2,1)S(1)} copy(bf16[128,8192]{1,0:T(8,128)(2,1)} %param.6) | data formatting | bytes 4194304 | tf_op args[0]
  11.1 2.9 %copy.9 = bf16[128,64,128]{2,0,1:T(8,128)(2,1)} copy(bf16[128,64,128]{0,2,1:T(8,128)(2,1)S(1)} %bitcast.37) | data formatting | bytes 4194304 | tf_op jit(solution)/shard_map/reshape | solution.py:42
  14.0 0.0 copy-start
  14.0 0.0 copy-start.5
  14.0 0.0 copy-start.6
  14.0 2.6 %gather_fusion.1 = bf16[64,128,128]{2,1,0:T(8,128)(2,1)S(1)} fusion(bf16[128,64,128]{2,0,1:T(8,128)(2,1)} %copy.9, s32[1024]{0:T(1024)S(1)} %pad_clamp_fusion.1), kind=kCustom, calls=%fused_computation.1 | custom fusion | bytes 4194560 | tf_op jit(solution)/shard_map/jit(_take)/gather | solution.py:43
  16.6 0.0 copy-done
  16.6 0.6 fusion.6
  17.2 0.0 copy-done.5
  17.2 0.0 copy-done.6
  17.3 0.7 iota_compare_fusion
  17.9 1.7 bitcast_select_fusion
  19.6 0.0 copy-start.4
  19.6 0.0 copy-start.3
  19.6 16.7 %all-to-all-start = ((bf16[64,128,128]{2,1,0:T(8,128)(2,1)}), bf16[64,128,128]{2,1,0:T(8,128)(2,1)S(1)}, u32[]{:S(2)}, u32[]{:S(2)}) async-start(bf16[64,128,128]{2,1,0:T(8,128)(2,1)} %bitcast_select_fusion), calls=%async_computation | async-start | bytes 4194304 | tf_op jit(solution)/shard_map/all_to_all | solution.py:48
  36.3 0.0 all-gather.2.cloned.1.call-start
  36.4 0.6 dynamic_slice.22
  37.0 0.0 copy-done.4
  37.0 13.4 %all_gather.6 = bf16[512,512]{1,0:T(8,128)(2,1)S(1)} all-gather(bf16[64,512]{1,0:T(8,128)(2,1)S(1)} %copy-done.4), channel_id=1, replica_groups=mesh['snode'=64,'rows'=8] {'rows'}, dimensions={0}, use_global_device_ids=true | all-gather | bytes 589824 | tf_op jit(solution)/shard_map/all_gather | solution.py:27
  50.4 0.0 copy-done.3
  50.4 1.5 convolution_convert_fusion.1
  52.0 0.0 copy-start.1
  52.0 0.0 all-gather.2.cloned.1.call-update
  52.0 0.0 all-reduce.2.cloned.1.call-start
  52.0 0.2 dynamic-slice_reduce_fusion
  52.2 0.6 gather_fusion
  52.9 36.3 %all-to-all-done = bf16[64,128,128]{2,1,0:T(8,128)(2,1)S(1)} async-done(((bf16[64,128,128]{2,1,0:T(8,128)(2,1)}), bf16[64,128,128]{2,1,0:T(8,128)(2,1)S(1)}, u32[]{:S(2)}, u32[]{:S(2)}) %all-to-all-start) | async-done | bytes 2097184 | tf_op jit(solution)/shard_map/all_to_all | solution.py:48
  89.2 0.6 gather_fusion.2
  89.8 0.1 broadcast_select_fusion
  89.9 11.6 %all_to_all.21 = bf16[8,128,128]{2,1,0:T(8,128)(2,1)S(1)} all-to-all(bf16[8,128,128]{2,1,0:T(8,128)(2,1)S(1)} %broadcast_select_fusion), channel_id=1, replica_groups=mesh['snode'=64,'rows'=8] {'rows'}, dimensions={0} | all-to-all | bytes 524288 | tf_op jit(solution)/shard_map/all_to_all | solution.py:52
  101.6 0.2 copy.10
  101.8 0.0 all-gather.2.cloned.1.call-done
  101.8 1.6 fusion
  103.3 0.0 copy-done.1
  103.4 0.0 copy-start.2
  103.4 1.1 convolution_convert_fusion
  104.5 0.0 all-reduce.2.cloned.1.call-update
  104.5 66.2 %all-reduce.2.cloned.1.call-done = bf16[512,512]{1,0:T(8,128)(2,1)} async-done(((bf16[512,512]{1,0:T(8,128)(2,1)}), bf16[512,512]{1,0:T(8,128)(2,1)}) %all-reduce.2.cloned.1.call-update) | async-done | bytes 524304 | tf_op jit(solution)/shard_map/psum | solution.py:62
  170.7 1.8 %convolution_subtract_fusion = f32[64,512]{1,0:T(8,128)} fusion(bf16[512,512]{1,0:T(8,128)(2,1)S(1)} %all_gather.6, s32[]{:T(128)S(6)} %select_n.116, bf16[512,512]{1,0:T(8,128)(2,1)} %all-reduce.2.cloned.1.call-done), kind=kOutput, calls=%fused_computation.9 | convolution fusion | flops 33619968 | bytes 852992 | tf_op jit(solution)/shard_map/dot_general | solution.py:30
  172.5 0.0 copy-done.2
  (6 shorter events, 0.0 us)
Async XLA Ops:
  14.0 2.6 %copy-start = (s32[64]{0:T(128)S(1)}, s32[64]{0:T(128)}, u32[]{:S(2)}) copy-start(s32[64]{0:T(128)} %param.9) | copy-start | bytes 772
  14.0 3.2 %copy-start.5 = (s32[64,8]{0,1:T(8,128)S(1)}, s32[64,8]{0,1:T(8,128)}, u32[]{:S(2)}) copy-start(s32[64,8]{0,1:T(8,128)} %param.7) | copy-start | bytes 6148
  14.0 3.2 %copy-start.6 = (s32[64]{0:T(128)S(1)}, s32[64]{0:T(128)}, u32[]{:S(2)}) copy-start(s32[64]{0:T(128)} %param.8) | copy-start | bytes 772
  19.6 17.4 %copy-start.4 = (bf16[64,512]{1,0:T(8,128)(2,1)S(1)}, bf16[64,512]{1,0:T(8,128)(2,1)}, u32[]{:S(2)}) copy-start(bf16[64,512]{1,0:T(8,128)(2,1)} %param.11) | copy-start | bytes 196612
  19.6 30.8 %copy-start.3 = (bf16[128,512]{1,0:T(8,128)(2,1)S(1)}, bf16[128,512]{1,0:T(8,128)(2,1)}, u32[]{:S(2)}) copy-start(bf16[128,512]{1,0:T(8,128)(2,1)} %param.10) | copy-start | bytes 393220
  19.6 69.6 %all-to-all-start = ((bf16[64,128,128]{2,1,0:T(8,128)(2,1)}), bf16[64,128,128]{2,1,0:T(8,128)(2,1)S(1)}, u32[]{:S(2)}, u32[]{:S(2)}) async-start(bf16[64,128,128]{2,1,0:T(8,128)(2,1)} %bitcast_select_fusion), calls=%async_computation | async-start | bytes 4194304 | tf_op jit(solution)/shard_map/all_to_all | solution.py:48
  36.3 65.5 %all-gather.2.cloned.1.call-start = ((), (), s32[]{:S(2)}) async-start(), calls=%async_computation.2 | async-start | bytes 1179648 | tf_op jit(solution)/shard_map/all_gather | solution.py:55
  52.0 51.4 %copy-start.1 = (bf16[128,512]{1,0:T(8,128)(2,1)S(1)}, bf16[128,512]{1,0:T(8,128)(2,1)}, u32[]{:S(2)}) copy-start(bf16[128,512]{1,0:T(8,128)(2,1)} %convolution_convert_fusion.1) | copy-start | bytes 393220
  52.0 118.7 %all-reduce.2.cloned.1.call-start = ((), (), s32[]{:S(2)}) async-start(), calls=%async_computation.3 | async-start | bytes 1048576 | tf_op jit(solution)/shard_map/psum | solution.py:62
  103.4 69.1 %copy-start.2 = (bf16[128,512]{1,0:T(8,128)(2,1)}, bf16[128,512]{1,0:T(8,128)(2,1)S(1)}, u32[]{:S(2)}) copy-start(bf16[128,512]{1,0:T(8,128)(2,1)S(1)} %fusion) | copy-start | bytes 393220
Sparse Core Ops, SparseCore 0:
  52.1 28.7 all-gather.1
  104.6 65.9 all-reduce.1
where the time goes:
time: 180 us; the launch traced here: 179 us
  waiting for transfers between devices  103 us (57%)
  blocking collectives  25.1 us (14%)
  starting transfers between devices  16.8 us (9%)
  between operations  14.2 us (8%)
  local copies, waits for them, and re-layouts  10.9 us (6%)
  matrix products  6 us (3%)
  other arithmetic  3.82 us (2%)
    psum x1, waiting for transfers between devices, per_device(): lax.psum(partial_diag.astype(jnp.bfloat16), 'rows').astype(jnp.float32)  66.2 us
    all_to_all x1, waiting for transfers between devices, per_device(): lax.all_to_all(outgoing, 'snode', split_axis=0, concat_axis=0, tiled=True)  36.3 us
    all_to_all x1, starting transfers between devices, per_device(): lax.all_to_all(outgoing, 'snode', split_axis=0, concat_axis=0, tiled=True)  16.7 us
    all_gather x1, blocking collectives, per_device(): piece = lax.all_gather(diag_inverse, 'rows', axis=0, tiled=True)  13.4 us
    all_to_all x1, blocking collectives, per_device(): lax.all_to_all(arranged, 'rows', split_axis=0, concat_axis=1, tiled=True)  11.6 us
  transfers between devices with their start and end apart: 3, of which 2 were waited for; matrix products, arithmetic and copies ran while one was open for 2% of the time, Pallas kernels for 0%

commit v1 on v0

--- a/solution.py
+++ b/solution.py
@@ -59,7 +59,9 @@
     partial_diag = lax.dot_general(
         u_factor, offdiag, (((0,), (0,)), ((), ())), preferred_element_type=jnp.float32
     )
-    whole_update = lax.psum(partial_diag.astype(jnp.bfloat16), "rows").astype(jnp.float32)
+    whole_update = jnp.sum(
+        lax.all_gather(partial_diag.astype(jnp.bfloat16), "rows"), axis=0
+    ).astype(jnp.float32)
     reduced = lax.dynamic_slice_in_dim(whole_update, band_start, band_rows, 0)
     return (offdiag, base_diag - reduced)
 

time: 180 us -> 149 us (0.83)
  the two profiles are of different devices: /device:TPU:8 before, /device:TPU:1 now
where the time goes in v1:
time: 149 us
  waiting for transfers between devices  65.6 us (44%)
  blocking collectives  28.9 us (19%)
  starting transfers between devices  17.4 us (12%)
  between operations  14.2 us (10%)
  local copies, waits for them, and re-layouts  10.9 us (7%)
  other arithmetic  6.87 us (5%)
  matrix products  5.19 us (3%)
    all_gather x1, waiting for transfers between devices, per_device(): lax.all_gather(partial_diag.astype(jnp.bfloat16), 'rows')  33.7 us
    all_to_all x1, waiting for transfers between devices, per_device(): lax.all_to_all(outgoing, 'snode', split_axis=0, concat_axis=0, tiled=True)  31.9 us
    all_to_all x1, starting transfers between devices, per_device(): lax.all_to_all(outgoing, 'snode', split_axis=0, concat_axis=0, tiled=True)  17.3 us
    all_to_all x1, blocking collectives, per_device(): lax.all_to_all(arranged, 'rows', split_axis=0, concat_axis=1, tiled=True)  14.6 us
    all_gather x1, blocking collectives, per_device(): piece = lax.all_gather(diag_inverse, 'rows', axis=0, tiled=True)  14.2 us
    unnamed x15, local copies, waits for them, and re-layouts  3.25 us
    reduce_sum x1, other arithmetic, per_device(): jnp.sum(lax.all_gather(partial_diag.astype(jnp.bfloat16), 'rows'), axis=0)  3.06 us
  transfers between devices with their start and end apart: 3, of which 2 were waited for; matrix products, arithmetic and copies ran while one was open for 3% of the time, Pallas kernels for 0%

profile of v1, /device:TPU:1, one launch (start us, length us, event | category | flops | bytes accessed | tf_op | source)
XLA Modules:
  0.0 149.0 jit_solution(2967641892347117014)
XLA Ops:
  7.2 0.7 and_bitcast_fusion
  7.9 3.2 %copy.8 = bf16[128,8192]{0,1:T(8,128)(2,1)S(1)} copy(bf16[128,8192]{1,0:T(8,128)(2,1)} %param.6) | data formatting | bytes 4194304 | tf_op args[0]
  11.1 2.9 %copy.9 = bf16[128,64,128]{2,0,1:T(8,128)(2,1)} copy(bf16[128,64,128]{0,2,1:T(8,128)(2,1)S(1)} %bitcast.38) | data formatting | bytes 4194304 | tf_op jit(solution)/shard_map/reshape | solution.py:42
  14.0 0.0 copy-start
  14.0 0.0 copy-start.5
  14.0 0.0 copy-start.6
  14.0 2.6 %gather_fusion.1 = bf16[64,128,128]{2,1,0:T(8,128)(2,1)S(1)} fusion(bf16[128,64,128]{2,0,1:T(8,128)(2,1)} %copy.9, s32[1024]{0:T(1024)S(1)} %pad_clamp_fusion.1), kind=kCustom, calls=%fused_computation.1 | custom fusion | bytes 4194560 | tf_op jit(solution)/shard_map/jit(_take)/gather | solution.py:43
  16.6 0.0 copy-done
  16.6 0.6 fusion.6
  17.2 0.0 copy-done.5
  17.2 0.0 copy-done.6
  17.3 0.7 iota_compare_fusion
  17.9 1.7 %bitcast_select_fusion = bf16[64,128,128]{2,1,0:T(8,128)(2,1)} fusion(bf16[64,128,128]{2,1,0:T(8,128)(2,1)S(1)} %gather_fusion.1, pred[64]{0:T(512)(128)(4,1)S(1)} %get-tuple-element.2, pred[64]{0:T(512)(128)(4,1)S(1)} %get-tuple-element.5), kind=kLoop, calls=%fused_computation.3 | loop fusion | flops 2097152 | bytes 4194432 | tf_op jit(solution)/shard_map/jit(_where)/select_n | solution.py:47
  19.6 0.0 copy-start.4
  19.6 0.0 copy-start.3
  19.6 17.3 %all-to-all-start = ((bf16[64,128,128]{2,1,0:T(8,128)(2,1)}), bf16[64,128,128]{2,1,0:T(8,128)(2,1)S(1)}, u32[]{:S(2)}, u32[]{:S(2)}) async-start(bf16[64,128,128]{2,1,0:T(8,128)(2,1)} %bitcast_select_fusion), calls=%async_computation | async-start | bytes 4194304 | tf_op jit(solution)/shard_map/all_to_all | solution.py:48
  36.9 0.0 all-gather.4.cloned.1.call-start
  36.9 0.6 dynamic_slice.22
  37.5 0.0 copy-done.4
  37.5 14.2 %all_gather.12 = bf16[512,512]{1,0:T(8,128)(2,1)S(1)} all-gather(bf16[64,512]{1,0:T(8,128)(2,1)S(1)} %copy-done.4), channel_id=1, replica_groups=mesh['snode'=64,'rows'=8] {'rows'}, dimensions={0}, use_global_device_ids=true | all-gather | bytes 589824 | tf_op jit(solution)/shard_map/all_gather | solution.py:27
  51.8 0.0 copy-done.3
  51.8 1.5 %convolution_convert_fusion.1 = bf16[128,512]{1,0:T(8,128)(2,1)} fusion(bf16[512,512]{1,0:T(8,128)(2,1)S(1)} %all_gather.12, bf16[128,512]{1,0:T(8,128)(2,1)S(1)} %copy-done.3, pred[]{:T(512)} %bitcast.12), kind=kOutput, calls=%fused_computation.7 | convolution fusion | flops 67239936 | bytes 786433 | tf_op jit(solution)/shard_map/dot_general | solution.py:28
  53.3 0.0 copy-start.1
  53.3 0.0 all-gather.4.cloned.1.call-update
  53.3 0.0 all-gather.6.cloned.1.call-start
  53.4 0.2 dynamic-slice_reduce_fusion
  53.6 0.6 gather_fusion
  54.3 31.9 %all-to-all-done = bf16[64,128,128]{2,1,0:T(8,128)(2,1)S(1)} async-done(((bf16[64,128,128]{2,1,0:T(8,128)(2,1)}), bf16[64,128,128]{2,1,0:T(8,128)(2,1)S(1)}, u32[]{:S(2)}, u32[]{:S(2)}) %all-to-all-start) | async-done | bytes 2097184 | tf_op jit(solution)/shard_map/all_to_all | solution.py:48
  86.2 0.6 gather_fusion.2
  86.8 0.1 broadcast_select_fusion
  86.9 14.6 %all_to_all.21 = bf16[8,128,128]{2,1,0:T(8,128)(2,1)S(1)} all-to-all(bf16[8,128,128]{2,1,0:T(8,128)(2,1)S(1)} %broadcast_select_fusion), channel_id=1, replica_groups=mesh['snode'=64,'rows'=8] {'rows'}, dimensions={0} | all-to-all | bytes 524288 | tf_op jit(solution)/shard_map/all_to_all | solution.py:52
  101.5 0.2 copy.10
  101.7 0.0 all-gather.4.cloned.1.call-done
  101.7 1.6 %fusion = bf16[128,512]{1,0:T(8,128)(2,1)S(1)} fusion(bf16[128,1024]{0,1:T(8,128)(2,1)S(1)} %bitcast.41, bf16[1024,512]{1,0:T(8,128)(2,1)} %all-gather.4.cloned.1.call-done), kind=kOutput, calls=%fused_computation.8 | convolution fusion | flops 134348800 | bytes 1441792 | tf_op jit(solution)/shard_map/dot_general | solution.py:53
  103.3 0.0 copy-done.1
  103.3 0.0 copy-start.2
  103.3 1.1 convolution_convert_fusion
  104.4 0.0 all-gather.6.cloned.1.call-update
  104.5 33.7 %all-gather.6.cloned.1.call-done = bf16[4096,512]{1,0:T(8,128)(2,1)} async-done(((bf16[512,512]{1,0:T(8,128)(2,1)}), bf16[4096,512]{1,0:T(8,128)(2,1)}) %all-gather.6.cloned.1.call-update) | async-done | bytes 4194320 | tf_op jit(solution)/shard_map/all_gather | solution.py:63
  138.1 3.1 %reduce_sum.22 = bf16[512,512]{1,0:T(8,128)(2,1)S(1)} reduce(bf16[8,512,512]{2,1,0:T(8,128)(2,1)} %bitcast.39, bf16[]{:T(256)} %constant.81.clone.1), dimensions={0}, to_apply=%region_2.3 | reduce | flops 1835008 | bytes 4718594 | tf_op jit(solution)/shard_map/reduce_sum | solution.py:62
  141.2 0.0 copy-done.2
  141.2 1.0 convolution_subtract_fusion
  (6 shorter events, 0.0 us)
Async XLA Ops:
  14.0 2.6 %copy-start = (s32[64]{0:T(128)S(1)}, s32[64]{0:T(128)}, u32[]{:S(2)}) copy-start(s32[64]{0:T(128)} %param.9) | copy-start | bytes 772
  14.0 3.2 %copy-start.5 = (s32[64,8]{0,1:T(8,128)S(1)}, s32[64,8]{0,1:T(8,128)}, u32[]{:S(2)}) copy-start(s32[64,8]{0,1:T(8,128)} %param.7) | copy-start | bytes 6148
  14.0 3.2 %copy-start.6 = (s32[64]{0:T(128)S(1)}, s32[64]{0:T(128)}, u32[]{:S(2)}) copy-start(s32[64]{0:T(128)} %param.8) | copy-start | bytes 772
  19.6 17.9 %copy-start.4 = (bf16[64,512]{1,0:T(8,128)(2,1)S(1)}, bf16[64,512]{1,0:T(8,128)(2,1)}, u32[]{:S(2)}) copy-start(bf16[64,512]{1,0:T(8,128)(2,1)} %param.11) | copy-start | bytes 196612
  19.6 32.2 %copy-start.3 = (bf16[128,512]{1,0:T(8,128)(2,1)S(1)}, bf16[128,512]{1,0:T(8,128)(2,1)}, u32[]{:S(2)}) copy-start(bf16[128,512]{1,0:T(8,128)(2,1)} %param.10) | copy-start | bytes 393220
  19.6 66.6 %all-to-all-start = ((bf16[64,128,128]{2,1,0:T(8,128)(2,1)}), bf16[64,128,128]{2,1,0:T(8,128)(2,1)S(1)}, u32[]{:S(2)}, u32[]{:S(2)}) async-start(bf16[64,128,128]{2,1,0:T(8,128)(2,1)} %bitcast_select_fusion), calls=%async_computation | async-start | bytes 4194304 | tf_op jit(solution)/shard_map/all_to_all | solution.py:48
  36.9 64.8 %all-gather.4.cloned.1.call-start = ((), (), s32[]{:S(2)}) async-start(), calls=%async_computation.2 | async-start | bytes 1179648 | tf_op jit(solution)/shard_map/all_gather | solution.py:55
  53.3 50.0 %copy-start.1 = (bf16[128,512]{1,0:T(8,128)(2,1)S(1)}, bf16[128,512]{1,0:T(8,128)(2,1)}, u32[]{:S(2)}) copy-start(bf16[128,512]{1,0:T(8,128)(2,1)} %convolution_convert_fusion.1) | copy-start | bytes 393220
  53.3 84.8 %all-gather.6.cloned.1.call-start = ((), (), s32[]{:S(2)}) async-start(), calls=%async_computation.3 | async-start | bytes 4718592 | tf_op jit(solution)/shard_map/all_gather | solution.py:63
  103.3 37.9 %copy-start.2 = (bf16[128,512]{1,0:T(8,128)(2,1)}, bf16[128,512]{1,0:T(8,128)(2,1)S(1)}, u32[]{:S(2)}) copy-start(bf16[128,512]{1,0:T(8,128)(2,1)S(1)} %fusion) | copy-start | bytes 393220
Sparse Core Ops, SparseCore 0:
  53.4 28.7 all-gather.3
  104.6 33.5 all-gather.5
